TPU v7x, 32 devices: a whole 2x2x4 slice. The times are simulated.
32 devices in a mesh: chan: 8 (over z, y), tm: 4 (over x, core).
Axes of the slice: x: 2, y: 2, z: 4, core: 2. Of those that a mesh axis runs over, the one named last changes fastest.
Arguments:
- record: bfloat16 [96, 2048], P('chan', 'tm'), may hold values from -6 to 6
- fir: float32 [96, 65], P('chan'), may hold values from -0.75 to 0.75
Outputs:
- xcorr: float32 [4, 96, 96, 256], P('tm', 'chan')
All inputs are finite; a program needn't handle non-finite values.
Results may differ from a plain program's by a relative error of at most 0.004.
Values may be sent and summed in bfloat16 or wider, within the bound.
A program may use at most 64 MiB of HBM per device.

v0:
```python
import math

import jax
import jax.numpy as jnp
from jax import lax
from jax.sharding import PartitionSpec as P

GROUP = 512
MAXLAG = 128


def extended_2(block, sides, width):
    for axis, dim in sides:
        count = lax.axis_size(axis)
        forward = [(i, i + 1) for i in range(count - 1)]
        backward = [(target, source) for source, target in forward]
        low = lax.ppermute(
            lax.slice_in_dim(block, block.shape[dim] - width, None, axis=dim), axis, forward
        )
        high = lax.ppermute(lax.slice_in_dim(block, 0, width, axis=dim), axis, backward)
        block = jnp.concatenate([low, block, high], axis=dim)
    return block


def whiten(widened_raw, fir, length):
    widened = widened_raw.astype(jnp.float32)
    running = jnp.zeros((widened.shape[0], length), jnp.float32)
    for k in range(fir.shape[1]):
        running = running + fir[:, k : k + 1] * widened[:, k : k + length]
    return running


def local(record, fir):
    ch_dev = record.shape[0]
    local_len = record.shape[1]
    half_width = (fir.shape[1] - 1) // 2
    lag_count = 2 * MAXLAG
    span = GROUP + lag_count
    factor = 1.0 / math.sqrt(GROUP)
    raw_ext = extended_2(record, (("tm", 1),), half_width)
    whitened = whiten(raw_ext, fir, local_len).astype(jnp.bfloat16)
    extended = extended_2(whitened, (("tm", 1),), MAXLAG)
    c = 0
    segment = extended[:, c * GROUP + MAXLAG : c * GROUP + MAXLAG + GROUP]
    padded = jnp.concatenate([segment, jnp.zeros((ch_dev, lag_count + 1), jnp.bfloat16)], axis=1)
    tiled = jnp.tile(padded, (1, lag_count))[:, : lag_count * span]
    expanded = [tiled.reshape(ch_dev, lag_count, span)]
    c = 0
    window = lax.all_gather(extended, "chan", axis=0, tiled=True)
    blocks = [
        jnp.einsum("amu,ju->ajm", expanded[c], window, preferred_element_type=jnp.float32) * factor
    ]
    return jnp.stack(blocks)


def solution(mesh):
    in_specs = (P("chan", "tm"), P("chan", None))
    out_specs = P("tm", "chan", None, None)
    return jax.shard_map(local, mesh=mesh, in_specs=in_specs, out_specs=out_specs, check_vma=False)
```

profile of v0, /device:TPU:6, one launch (start us, length us, event | category | flops | bytes accessed | tf_op | source)
XLA Modules:
  0.0 80.0 jit_solution(231138366995109417)
XLA Ops:
  0.0 0.8 fusion.74
  0.8 1.9 %collective-permute-start = (bf16[12,32]{1,0:T(8,128)(2,1)S(1)}, bf16[12,32]{1,0:T(8,128)(2,1)S(1)}, u32[]{:S(2)}, u32[]{:S(2)}) collective-permute-start(bf16[12,32]{1,0:T(8,128)(2,1)S(1)} %get-tuple-element.72), channel_id=1, source_target_pairs={{0,1},{1,2},{2,3},{4,5},{5,6},{6,7},{8,9},{9,10},{10,11},{12,13},{... | collective-permute-start | bytes 2312 | tf_op jit(solution)/shard_map/ppermute | solution.py:17
  2.7 3.6 %collective-permute-start.1 = (bf16[12,32]{1,0:T(8,128)(2,1)S(1)}, bf16[12,32]{1,0:T(8,128)(2,1)S(1)}, u32[]{:S(2)}, u32[]{:S(2)}) collective-permute-start(bf16[12,32]{1,0:T(8,128)(2,1)S(1)} %get-tuple-element.73), channel_id=1, source_target_pairs={{1,0},{2,1},{3,2},{5,4},{6,5},{7,6},{9,8},{10,9},{11,10},{13,12},{... | collective-permute-start | bytes 2312 | tf_op jit(solution)/shard_map/ppermute | solution.py:20
  6.3 1.9 %slice_reduce_fusion.64 = (f32[12]{0:T(128)S(1)}, f32[12]{0:T(128)S(1)}, f32[12]{0:T(128)S(1)}, f32[12]{0:T(128)S(1)}, f32[12]{0:T(128)S(1)}, /*index=5*/f32[12]...) fusion(f32[12,65]{1,0:T(8,128)} %param.3), kind=kLoop, calls=%fused_computation.200 | loop fusion | bytes 1824 | tf_op jit(solution)/shard_map/slice | solution.py:29
  8.3 1.9 %slice_reduce_fusion.63 = (f32[12]{0:T(128)S(1)}, f32[12]{0:T(128)S(1)}, f32[12]{0:T(128)S(1)}, f32[12]{0:T(128)S(1)}, f32[12]{0:T(128)S(1)}, /*index=5*/f32[12]...) fusion(f32[12,65]{1,0:T(8,128)} %param.3), kind=kLoop, calls=%fused_computation.199 | loop fusion | bytes 1824 | tf_op jit(solution)/shard_map/slice | solution.py:29
  10.2 1.9 %slice_reduce_fusion.62 = (f32[12]{0:T(128)S(1)}, f32[12]{0:T(128)S(1)}, f32[12]{0:T(128)S(1)}, f32[12]{0:T(128)S(1)}, f32[12]{0:T(128)S(1)}, /*index=5*/f32[12]...) fusion(f32[12,65]{1,0:T(8,128)} %param.3), kind=kLoop, calls=%fused_computation.198 | loop fusion | bytes 1824 | tf_op jit(solution)/shard_map/slice | solution.py:29
  12.1 1.3 %slice_reduce_fusion.61 = (f32[12]{0:T(128)S(1)}, f32[12]{0:T(128)S(1)}, f32[12]{0:T(128)S(1)}, f32[12]{0:T(128)S(1)}, f32[12]{0:T(128)S(1)}, /*index=5*/f32[12]{0:T(128)S(1)}, f32[12]{0:T(128)S(1)}, f32[12]{0:T(128)S(1)}) fusion(f32[12,65]{1,0:T(8,128)} %param.3), kind=kLoop, calls=%fused_computation.197 | loop fusion | bytes 768 | tf_op jit(solution)/shard_map/slice | solution.py:29
  13.4 0.0 collective-permute-done
  13.5 0.0 collective-permute-done.1
  13.5 0.8 maximum_convert_fusion
  14.3 0.8 fusion.9
  15.1 1.9 %collective-permute-start.2 = (bf16[12,128]{1,0:T(8,128)(2,1)S(1)}, bf16[12,128]{1,0:T(8,128)(2,1)S(1)}, u32[]{:S(2)}, u32[]{:S(2)}) collective-permute-start(bf16[12,128]{1,0:T(8,128)(2,1)S(1)} %get-tuple-element.70), channel_id=1, source_target_pairs={{0,1},{1,2},{2,3},{4,5},{5,6},{6,7},{8,9},{9,10},{10,11},{12,13},{... | collective-permute-start | bytes 9224 | tf_op jit(solution)/shard_map/ppermute | solution.py:17
  17.0 3.6 %collective-permute-start.3 = (bf16[12,128]{1,0:T(8,128)(2,1)S(1)}, bf16[12,128]{1,0:T(8,128)(2,1)S(1)}, u32[]{:S(2)}, u32[]{:S(2)}) collective-permute-start(bf16[12,128]{1,0:T(8,128)(2,1)S(1)} %get-tuple-element.71), channel_id=1, source_target_pairs={{1,0},{2,1},{3,2},{5,4},{6,5},{7,6},{9,8},{10,9},{11,10},{13,12},{... | collective-permute-start | bytes 9224 | tf_op jit(solution)/shard_map/ppermute | solution.py:20
  20.7 2.9 %tile.4 = bf16[12,256,769]{2,1,0:T(8,128)(2,1)} broadcast(bf16[12,769]{1,0:T(8,128)(2,1)S(1)} %concatenate.11), dimensions={0,2} | broadcast | bytes 4743192 | tf_op jit(solution)/shard_map/tile | solution.py:46
  23.5 13.6 %tile.10 = bf16[12,196864]{1,0:T(8,128)(2,1)} reshape(bf16[12,256,769]{2,1,0:T(8,128)(2,1)} %tile.4) | data formatting | bytes 9449472 | tf_op jit(solution)/shard_map/tile | solution.py:46
  37.1 0.0 slice-start
  37.1 2.8 %slice-done = bf16[12,196608]{1,0:T(8,128)(2,1)S(1)} async-done(((bf16[12,196864]{1,0:T(8,128)(2,1)}), bf16[12,196608]{1,0:T(8,128)(2,1)S(1)}, s32[]{:S(2)}) %slice-start) | async-done | bytes 4718616 | tf_op jit(solution)/shard_map/slice | solution.py:46
  39.9 4.1 %copy.3 = bf16[2,8,256,768]{3,2,1,0:T(8,128)(2,1)} copy(bf16[2,8,256,768]{3,1,2,0:T(8,128)(2,1)S(1)} %bitcast.10) | data formatting | bytes 12582912
  44.0 0.0 collective-permute-done.2
  44.0 0.0 collective-permute-done.3
  44.0 31.0 %all-gather = bf16[8,12,768]{2,1,0:T(8,128)(2,1)S(1)} all-gather(bf16[1,12,768]{2,1,0:T(8,128)(2,1)S(1)} %maximum_bitcast_fusion), channel_id=1, replica_groups=mesh['chan'=8,'tm'=4] {'chan'}, dimensions={0}, use_global_device_ids=true | all-gather | bytes 165888 | tf_op jit(solution)/shard_map/all_gather | solution.py:49
  75.1 4.9 %fusion.5 = f32[1,12,96,256]{3,2,1,0:T(8,128)} fusion(bf16[96,768,1]{1,0,2:T(8,128)(2,1)S(1)} %reshape.10, bf16[16,256,768]{2,1,0:T(8,128)(2,1)} %bitcast.11), kind=kOutput, calls=%fused_computation.3 | convolution fusion | flops 453279744 | bytes 6045696 | tf_op jit(solution)/shard_map/amu,ju->ajm/dot_general | solution.py:51
  (4 shorter events, 0.1 us)
Async XLA Ops:
  0.8 12.7 %collective-permute-start = (bf16[12,32]{1,0:T(8,128)(2,1)S(1)}, bf16[12,32]{1,0:T(8,128)(2,1)S(1)}, u32[]{:S(2)}, u32[]{:S(2)}) collective-permute-start(bf16[12,32]{1,0:T(8,128)(2,1)S(1)} %get-tuple-element.72), channel_id=1, source_target_pairs={{0,1},{1,2},{2,3},{4,5},{5,6},{6,7},{8,9},{9,10},{10,11},{12,13},{... | collective-permute-start | bytes 2312 | tf_op jit(solution)/shard_map/ppermute | solution.py:17
  2.7 10.8 %collective-permute-start.1 = (bf16[12,32]{1,0:T(8,128)(2,1)S(1)}, bf16[12,32]{1,0:T(8,128)(2,1)S(1)}, u32[]{:S(2)}, u32[]{:S(2)}) collective-permute-start(bf16[12,32]{1,0:T(8,128)(2,1)S(1)} %get-tuple-element.73), channel_id=1, source_target_pairs={{1,0},{2,1},{3,2},{5,4},{6,5},{7,6},{9,8},{10,9},{11,10},{13,12},{... | collective-permute-start | bytes 2312 | tf_op jit(solution)/shard_map/ppermute | solution.py:20
  15.1 28.9 %collective-permute-start.2 = (bf16[12,128]{1,0:T(8,128)(2,1)S(1)}, bf16[12,128]{1,0:T(8,128)(2,1)S(1)}, u32[]{:S(2)}, u32[]{:S(2)}) collective-permute-start(bf16[12,128]{1,0:T(8,128)(2,1)S(1)} %get-tuple-element.70), channel_id=1, source_target_pairs={{0,1},{1,2},{2,3},{4,5},{5,6},{6,7},{8,9},{9,10},{10,11},{12,13},{... | collective-permute-start | bytes 9224 | tf_op jit(solution)/shard_map/ppermute | solution.py:17
  17.0 27.0 %collective-permute-start.3 = (bf16[12,128]{1,0:T(8,128)(2,1)S(1)}, bf16[12,128]{1,0:T(8,128)(2,1)S(1)}, u32[]{:S(2)}, u32[]{:S(2)}) collective-permute-start(bf16[12,128]{1,0:T(8,128)(2,1)S(1)} %get-tuple-element.71), channel_id=1, source_target_pairs={{1,0},{2,1},{3,2},{5,4},{6,5},{7,6},{9,8},{10,9},{11,10},{13,12},{... | collective-permute-start | bytes 9224 | tf_op jit(solution)/shard_map/ppermute | solution.py:20
  37.1 2.8 %slice-start = ((bf16[12,196864]{1,0:T(8,128)(2,1)}), bf16[12,196608]{1,0:T(8,128)(2,1)S(1)}, s32[]{:S(2)}) async-start(bf16[12,196864]{1,0:T(8,128)(2,1)} %tile.10), calls=%async_computation | async-start | bytes 12582912 | tf_op jit(solution)/shard_map/slice | solution.py:46
where the time goes:
time: 80.6 us; the launch traced here: 80 us
  local copies, waits for them, and re-layouts  31.2 us (39%)
  blocking collectives  31 us (38%)
  starting transfers between devices  11.1 us (14%)
  matrix products  4.89 us (6%)
  other arithmetic  1.59 us (2%)
    all_gather x1, blocking collectives, local(): window = lax.all_gather(extended, 'chan', axis=0, tiled=True)  31 us
    another operation x2, local copies, waits for them, and re-layouts, local(): tiled = jnp.tile(padded, (1, lag_count))[:, :lag_count * span]  16.5 us
    ppermute x2, starting transfers between devices, extended_2(): lax.ppermute(lax.slice_in_dim(block, 0, width, axis=dim), axis, backward)  7.28 us
    slice x4, local copies, waits for them, and re-layouts, whiten(): running = running + fir[:, k:k + 1] * widened[:, k:k + length]  7.1 us
    dot_general x1, matrix products, local(): jnp.einsum('amu,ju->ajm', expanded[c], window, preferred_element_type=jnp...  4.89 us
    unnamed x2, local copies, waits for them, and re-layouts  4.09 us
    ppermute x2, starting transfers between devices, extended_2(): lax.ppermute(lax.slice_in_dim(block, block.shape[dim] - width, None, axis...  3.83 us
    slice x2, local copies, waits for them, and re-layouts, local(): tiled = jnp.tile(padded, (1, lag_count))[:, :lag_count * span]  2.78 us
  transfers between devices with their start and end apart: 4, of which 0 were waited for; matrix products, arithmetic and copies ran while one was open for 35% of the time, Pallas kernels for 0%

commit v1 on v0

v1 whole, which is shorter than its diff:
```python
import math

import jax
import jax.numpy as jnp
from jax import lax
from jax.experimental import pallas as pl
from jax.experimental.pallas import tpu as pltpu
from jax.sharding import PartitionSpec as P

GROUP = 512
MAXLAG = 128
LAGS = 2 * MAXLAG
SPAN = GROUP + LAGS
BAND = GROUP + MAXLAG
HALO = 256
MESH = pl.DeviceIdType.MESH


def whiten(x, fir, first, length):
    taps = fir.shape[1]
    width = -(-(length + taps) // 128) * 128
    x = x[:, first : first + width]
    steps = 8
    moved = [x if b == 0 else pltpu.roll(x, width - b, 1) for b in range(steps)]
    total = None
    for a in range(0, taps, steps):
        part = None
        for b in range(min(steps, taps - a)):
            term = fir[:, a + b : a + b + 1] * moved[b]
            part = term if part is None else part + term
        if a:
            part = pltpu.roll(part, width - a, 1)
        total = part if total is None else total + part
    return total[:, :length]


def gather_kernel(record, fir, gathered, low, high, own, halo_send, halo_recv, send, recv):
    n, tn = lax.axis_size("chan"), lax.axis_size("tm")
    me, tm = lax.axis_index("chan"), lax.axis_index("tm")
    right, left = lax.rem(tm + 1, tn), lax.rem(tm + tn - 1, tn)
    length = record.shape[1]

    barrier = pltpu.get_barrier_semaphore()
    for t in (left, right):
        pl.semaphore_signal(barrier, inc=1, device_id=(me, t), device_id_type=MESH)
    for d in range(1, n):
        pl.semaphore_signal(
            barrier, inc=1, device_id=(lax.rem(me + d, n), tm), device_id_type=MESH
        )
    pl.semaphore_wait(barrier, n + 1)

    to_right = pltpu.make_async_remote_copy(
        record.at[:, length - HALO :], low, halo_send.at[0], halo_recv.at[0],
        device_id=(me, right), device_id_type=MESH,
    )
    to_left = pltpu.make_async_remote_copy(
        record.at[:, :HALO], high, halo_send.at[1], halo_recv.at[1],
        device_id=(me, left), device_id_type=MESH,
    )
    to_right.start()
    to_left.start()
    to_right.wait()
    to_left.wait()

    before = jnp.where(tm > 0, low[...].astype(jnp.float32), 0.0)
    after = jnp.where(tm < tn - 1, high[...].astype(jnp.float32), 0.0)
    x = jnp.concatenate([before, record[...].astype(jnp.float32), after], axis=1)
    half = (fir.shape[1] - 1) // 2
    y = whiten(pltpu.roll(x, x.shape[1] - (HALO - MAXLAG - half), 1), fir[...], 0, SPAN)
    at = lax.broadcasted_iota(jnp.int32, y.shape, 1) + (tm * GROUP - MAXLAG)
    y = jnp.where((at >= 0) & (at < tn * GROUP), y, 0.0).astype(jnp.bfloat16)
    own[...] = y
    gathered[me] = y

    copies = []
    for d in range(1, n):
        copy = pltpu.make_async_remote_copy(
            own, gathered.at[me], send.at[d - 1], recv.at[d - 1],
            device_id=(lax.rem(me + d, n), tm), device_id_type=MESH,
        )
        copy.start()
        copies.append(copy)
    for copy in copies:
        copy.wait()


def correlate_kernel(gathered, out, wide, lead, band, result, sem):
    n, ch = gathered.shape[0], gathered.shape[1]
    rows = n * ch
    me = lax.axis_index("chan")
    factor = 1.0 / math.sqrt(GROUP)
    for c in range(n):
        wide[c * ch : (c + 1) * ch, :] = gathered[c].astype(jnp.float32)
    lead[:, :GROUP] = gathered[me][:, MAXLAG : MAXLAG + GROUP].astype(jnp.float32)
    lead[:, GROUP:] = jnp.zeros((ch, MAXLAG), jnp.float32)
    w = wide[...].astype(jnp.bfloat16)
    both = jnp.concatenate([w[:, :BAND], w[:, MAXLAG:]], axis=0)
    copies = []
    for p in range(ch // 2):
        for s in range(2):
            line = jnp.broadcast_to(lead[2 * p + s : 2 * p + s + 1, :], (MAXLAG, BAND))
            moved = pltpu.roll(line, 0, 1, stride=1, stride_axis=0)
            band[s * MAXLAG : (s + 1) * MAXLAG, :] = moved.astype(jnp.bfloat16)
        r = lax.dot_general(
            both, band[...], (((1,), (1,)), ((), ())), preferred_element_type=jnp.float32
        ) * factor
        for s in range(2):
            for h in range(2):
                result[2 * p + s, :, h * MAXLAG : (h + 1) * MAXLAG] = r[
                    h * rows : (h + 1) * rows, s * MAXLAG : (s + 1) * MAXLAG
                ]
        copy = pltpu.make_async_copy(
            result.at[2 * p : 2 * p + 2], out.at[0, 2 * p : 2 * p + 2], sem.at[p]
        )
        copy.start()
        copies.append(copy)
    for copy in copies:
        copy.wait()


def local(record, fir):
    ch = record.shape[0]
    n = lax.axis_size("chan")
    vmem = pl.BlockSpec(memory_space=pltpu.VMEM)
    gathered = pl.pallas_call(
        gather_kernel,
        out_shape=jax.ShapeDtypeStruct((n, ch, SPAN), jnp.bfloat16),
        in_specs=[vmem, vmem],
        out_specs=vmem,
        scratch_shapes=[
            pltpu.VMEM((ch, HALO), jnp.bfloat16),
            pltpu.VMEM((ch, HALO), jnp.bfloat16),
            pltpu.VMEM((ch, SPAN), jnp.bfloat16),
            pltpu.SemaphoreType.DMA((2,)),
            pltpu.SemaphoreType.DMA((2,)),
            pltpu.SemaphoreType.DMA((n - 1,)),
            pltpu.SemaphoreType.DMA((n - 1,)),
        ],
        compiler_params=pltpu.CompilerParams(collective_id=0, has_side_effects=True),
    )(record, fir)
    return pl.pallas_call(
        correlate_kernel,
        out_shape=jax.ShapeDtypeStruct((1, ch, n * ch, LAGS), jnp.float32),
        in_specs=[vmem],
        out_specs=pl.BlockSpec(memory_space=pl.ANY),
        scratch_shapes=[
            pltpu.VMEM((n * ch, SPAN), jnp.float32),
            pltpu.VMEM((ch, BAND), jnp.float32),
            pltpu.VMEM((2 * MAXLAG, BAND), jnp.bfloat16),
            pltpu.VMEM((ch, n * ch, LAGS), jnp.float32),
            pltpu.SemaphoreType.DMA((ch // 2,)),
        ],
    )(gathered)


def solution(mesh):
    in_specs = (P("chan", "tm"), P("chan", None))
    out_specs = P("tm", "chan", None, None)
    return jax.shard_map(local, mesh=mesh, in_specs=in_specs, out_specs=out_specs, check_vma=False)
```

time: 80.6 us -> 18.1 us (0.22)
  the two profiles are of different devices: /device:TPU:6 before, /device:TPU:0 now
where the time goes in v1:
time: 18.1 us; the launch traced here: 17.8 us
  Pallas kernels  17.8 us (98%)
    pallas_call x1, Pallas kernels, local(): pl.pallas_call(gather_kernel, out_shape=jax.ShapeDtypeStruct((n, ch, SPAN...  15.1 us
    pallas_call x1, Pallas kernels, local(): pl.pallas_call(correlate_kernel, out_shape=jax.ShapeDtypeStruct((1, ch, n...  2.71 us

profile of v1, /device:TPU:0, one launch (start us, length us, event | category | flops | bytes accessed | tf_op | source)
XLA Modules:
  0.0 17.8 jit_solution(10934409960614408304)
XLA Ops:
  0.0 15.1 %shard_map.28.gathered = bf16[8,12,768]{2,1,0:T(8,128)(2,1)} custom-call(bf16[12,512]{1,0:T(8,128)(2,1)} %record.1, f32[12,65]{1,0:T(8,128)} %fir.1), custom_call_target="tpu_custom_call" | custom-call | tf_op jit(solution)/shard_map/pallas_call | solution.py:125
  15.1 2.7 %shard_map.29 = f32[1,12,96,256]{3,2,1,0:T(8,128)} custom-call(bf16[8,12,768]{2,1,0:T(8,128)(2,1)} %shard_map.28.gathered), custom_call_target="tpu_custom_call" | custom-call | tf_op jit(solution)/shard_map/pallas_call | solution.py:141

commit v2 on v1

v2 whole, which is shorter than its diff:
```python
import math

import jax
import jax.numpy as jnp
from jax import lax
from jax.experimental import pallas as pl
from jax.experimental.pallas import tpu as pltpu
from jax.sharding import PartitionSpec as P

GROUP = 512
MAXLAG = 128
LAGS = 2 * MAXLAG
SPAN = GROUP + LAGS
BAND = GROUP + MAXLAG
HALO = 256
MESH = pl.DeviceIdType.MESH


def whiten(x, fir, first, length):
    taps = fir.shape[1]
    width = -(-(length + taps) // 128) * 128
    x = x[:, first : first + width]
    steps = 8
    moved = [x if b == 0 else pltpu.roll(x, width - b, 1) for b in range(steps)]
    total = None
    for a in range(0, taps, steps):
        part = None
        for b in range(min(steps, taps - a)):
            term = fir[:, a + b : a + b + 1] * moved[b]
            part = term if part is None else part + term
        if a:
            part = pltpu.roll(part, width - a, 1)
        total = part if total is None else total + part
    return total[:, :length]


def pack(y):
    return jnp.concatenate(
        [y[:, k : k + 128] for k in range(0, y.shape[1], 128)], axis=0
    ).astype(jnp.bfloat16)


def gather_kernel(record_hbm, fir_hbm, wide, bands, record, fir, low, high, own, blocks,
                  load, halo_send, halo_recv, send, recv):
    n, tn = lax.axis_size("chan"), lax.axis_size("tm")
    me, tm = lax.axis_index("chan"), lax.axis_index("tm")
    right, left = lax.rem(tm + 1, tn), lax.rem(tm + tn - 1, tn)
    ch, length = record.shape

    barrier = pltpu.get_barrier_semaphore()
    for d in range(n - 1, 0, -1):
        pl.semaphore_signal(
            barrier, inc=1, device_id=(lax.rem(me + d, n), tm), device_id_type=MESH
        )
    for t in (left, right):
        pl.semaphore_signal(barrier, inc=1, device_id=(me, t), device_id_type=MESH)
    get_record = pltpu.make_async_copy(record_hbm, record, load.at[0])
    get_fir = pltpu.make_async_copy(fir_hbm, fir, load.at[1])
    get_record.start()
    get_fir.start()
    get_record.wait()
    get_fir.wait()
    pl.semaphore_wait(barrier, n + 1)

    to_right = pltpu.make_async_remote_copy(
        record.at[:, length - HALO :], low, halo_send.at[0], halo_recv.at[0],
        device_id=(me, right), device_id_type=MESH,
    )
    to_left = pltpu.make_async_remote_copy(
        record.at[:, :HALO], high, halo_send.at[1], halo_recv.at[1],
        device_id=(me, left), device_id_type=MESH,
    )
    to_right.start()
    to_left.start()
    to_right.wait_recv()
    to_left.wait_recv()

    before = jnp.where(tm > 0, low[...].astype(jnp.float32), 0.0)
    after = jnp.where(tm < tn - 1, high[...].astype(jnp.float32), 0.0)
    x = jnp.concatenate([before, record[...].astype(jnp.float32), after], axis=1)
    half = (fir.shape[1] - 1) // 2
    y = whiten(pltpu.roll(x, x.shape[1] - (HALO - MAXLAG - half), 1), fir[...], 0, SPAN)
    at = lax.broadcasted_iota(jnp.int32, y.shape, 1) + (tm * GROUP - MAXLAG)
    y = jnp.where((at >= 0) & (at < tn * GROUP), y, 0.0)
    y = y.astype(jnp.bfloat16).astype(jnp.float32)
    own[...] = pack(y)

    copies = []
    for d in range(1, n):
        copy = pltpu.make_async_remote_copy(
            own, blocks.at[me], send.at[d - 1], recv.at[me],
            device_id=(lax.rem(me + d, n), tm), device_id_type=MESH,
        )
        copy.start()
        copies.append(copy)
    blocks[me] = own[...]

    lead = jnp.concatenate(
        [y[:, MAXLAG : MAXLAG + GROUP], jnp.zeros((ch, MAXLAG), jnp.float32)], axis=1
    )
    for i in range(ch):
        line = jnp.broadcast_to(lead[i : i + 1, :], (MAXLAG, BAND))
        moved = pltpu.roll(line, 0, 1, stride=1, stride_axis=0)
        bands[i * MAXLAG : (i + 1) * MAXLAG, :] = moved.astype(jnp.bfloat16)

    for c in range(n):
        @pl.when(me != c)
        def _():
            pltpu.make_async_remote_copy(
                own, blocks.at[c], send.at[0], recv.at[c],
                device_id=(c, tm), device_id_type=MESH,
            ).wait_recv()

        block = blocks[c].astype(jnp.float32)
        for k in range(SPAN // 128):
            wide[c * ch : (c + 1) * ch, k * 128 : (k + 1) * 128] = block[k * ch : (k + 1) * ch, :]
    to_right.wait_send()
    to_left.wait_send()
    for copy in copies:
        copy.wait_send()


def correlate_kernel(wide, bands, out, result, sem):
    rows = wide.shape[0]
    ch = bands.shape[0] // MAXLAG
    factor = 1.0 / math.sqrt(GROUP)
    w = wide[...].astype(jnp.bfloat16)
    both = jnp.concatenate([w[:, :BAND], w[:, MAXLAG:]], axis=0)
    copies = []
    for p in range(ch // 2):
        r = lax.dot_general(
            both, bands[p * LAGS : (p + 1) * LAGS, :], (((1,), (1,)), ((), ())),
            preferred_element_type=jnp.float32,
        ) * factor
        for s in range(2):
            for h in range(2):
                result[2 * p + s, :, h * MAXLAG : (h + 1) * MAXLAG] = r[
                    h * rows : (h + 1) * rows, s * MAXLAG : (s + 1) * MAXLAG
                ]
        copy = pltpu.make_async_copy(
            result.at[2 * p : 2 * p + 2], out.at[0, 2 * p : 2 * p + 2], sem.at[p]
        )
        copy.start()
        copies.append(copy)
    for copy in copies:
        copy.wait()


def local(record, fir):
    ch, length = record.shape
    n = lax.axis_size("chan")
    vmem = pl.BlockSpec(memory_space=pltpu.VMEM)
    hbm = pl.BlockSpec(memory_space=pltpu.HBM)
    packed = ch * (SPAN // 128)
    wide, bands = pl.pallas_call(
        gather_kernel,
        out_shape=(
            pltpu.VMEM((n * ch, SPAN), jnp.float32),
            pltpu.VMEM((ch * MAXLAG, BAND), jnp.bfloat16),
        ),
        in_specs=[hbm, hbm],
        out_specs=(vmem, vmem),
        scratch_shapes=[
            pltpu.VMEM((ch, length), jnp.bfloat16),
            pltpu.VMEM(fir.shape, jnp.float32),
            pltpu.VMEM((ch, HALO), jnp.bfloat16),
            pltpu.VMEM((ch, HALO), jnp.bfloat16),
            pltpu.VMEM((packed, 128), jnp.bfloat16),
            pltpu.VMEM((n, packed, 128), jnp.bfloat16),
            pltpu.SemaphoreType.DMA((2,)),
            pltpu.SemaphoreType.DMA((2,)),
            pltpu.SemaphoreType.DMA((2,)),
            pltpu.SemaphoreType.DMA((n - 1,)),
            pltpu.SemaphoreType.DMA((n,)),
        ],
        compiler_params=pltpu.CompilerParams(
            collective_id=0, has_side_effects=True, vmem_limit_bytes=16 << 20
        ),
    )(*(pltpu.with_memory_space_constraint(x, pltpu.HBM) for x in (record, fir)))
    return pl.pallas_call(
        correlate_kernel,
        out_shape=jax.ShapeDtypeStruct((1, ch, n * ch, LAGS), jnp.float32),
        in_specs=[vmem, vmem],
        out_specs=pl.BlockSpec(memory_space=pl.ANY),
        scratch_shapes=[
            pltpu.VMEM((ch, n * ch, LAGS), jnp.float32),
            pltpu.SemaphoreType.DMA((ch // 2,)),
        ],
        compiler_params=pltpu.CompilerParams(vmem_limit_bytes=16 << 20),
    )(wide, bands)


def solution(mesh):
    in_specs = (P("chan", "tm"), P("chan", None))
    out_specs = P("tm", "chan", None, None)
    return jax.shard_map(local, mesh=mesh, in_specs=in_specs, out_specs=out_specs, check_vma=False)
```

time: 18.1 us -> 15.1 us (0.83)
  Pallas kernels: 17.8 us -> 14.9 us
    pallas_call x1, Pallas kernels: 15.1 us -> 13.3 us  [local(): pl.pallas_call(gather_kernel, out_shape=(pltpu.VMEM((n * ch, SPAN), jnp.f...]
    pallas_call x1, Pallas kernels: 2.71 us -> 1.63 us  [local(): pl.pallas_call(correlate_kernel, out_shape=jax.ShapeDtypeStruct((1, ch, n...]
where the time goes in v2:
time: 15.1 us; the launch traced here: 14.9 us
  Pallas kernels  14.9 us (99%)
    pallas_call x1, Pallas kernels, local(): pl.pallas_call(gather_kernel, out_shape=(pltpu.VMEM((n * ch, SPAN), jnp.f...  13.3 us
    pallas_call x1, Pallas kernels, local(): pl.pallas_call(correlate_kernel, out_shape=jax.ShapeDtypeStruct((1, ch, n...  1.63 us

profile of v2, /device:TPU:0, one launch (start us, length us, event | category | flops | bytes accessed | tf_op | source)
XLA Modules:
  0.0 14.9 jit_solution(8808093599351195604)
XLA Ops:
  0.0 13.3 %shard_map.28 = (f32[96,768]{1,0:T(8,128)S(1)}, bf16[1536,640]{1,0:T(8,128)(2,1)S(1)}) custom-call(bf16[12,512]{1,0:T(8,128)(2,1)} %record_hbm.1, f32[12,65]{1,0:T(8,128)} %fir_hbm.1), custom_call_target="tpu_custom_call" | custom-call | tf_op jit(solution)/shard_map/pallas_call | solution.py:155
  13.3 1.6 %shard_map.29 = f32[1,12,96,256]{3,2,1,0:T(8,128)} custom-call(f32[96,768]{1,0:T(8,128)S(1)} %get-tuple-element.7.wide, bf16[1536,640]{1,0:T(8,128)(2,1)S(1)} %get-tuple-element.8.bands), custom_call_target="tpu_custom_call" | custom-call | tf_op jit(solution)/shard_map/pallas_call | solution.py:180

commit v3 on v2

--- a/solution.py
+++ b/solution.py
@@ -16,17 +16,16 @@
 MESH = pl.DeviceIdType.MESH
 
 
-def whiten(x, fir, first, length):
-    taps = fir.shape[1]
-    width = -(-(length + taps) // 128) * 128
-    x = x[:, first : first + width]
+def whiten(x, taps, width, length):
+    count = taps.shape[1]
+    x = x[:, :width]
     steps = 8
     moved = [x if b == 0 else pltpu.roll(x, width - b, 1) for b in range(steps)]
     total = None
-    for a in range(0, taps, steps):
+    for a in range(0, count, steps):
         part = None
-        for b in range(min(steps, taps - a)):
-            term = fir[:, a + b : a + b + 1] * moved[b]
+        for b in range(min(steps, count - a)):
+            term = taps[:, a + b : a + b + 1] * moved[b]
             part = term if part is None else part + term
         if a:
             part = pltpu.roll(part, width - a, 1)
@@ -41,58 +40,113 @@
 
 
 def gather_kernel(record_hbm, fir_hbm, wide, bands, record, fir, low, high, own, blocks,
-                  load, halo_send, halo_recv, send, recv):
+                  load, halo_send, halo_recv, send, recv, near, ready):
     n, tn = lax.axis_size("chan"), lax.axis_size("tm")
     me, tm = lax.axis_index("chan"), lax.axis_index("tm")
-    right, left = lax.rem(tm + 1, tn), lax.rem(tm + tn - 1, tn)
     ch, length = record.shape
 
+    first, last = tm == 0, tm == tn - 1
+
     barrier = pltpu.get_barrier_semaphore()
-    for d in range(n - 1, 0, -1):
-        pl.semaphore_signal(
-            barrier, inc=1, device_id=(lax.rem(me + d, n), tm), device_id_type=MESH
-        )
-    for t in (left, right):
-        pl.semaphore_signal(barrier, inc=1, device_id=(me, t), device_id_type=MESH)
+    for c in range(1, n):
+        @pl.when(me < c)
+        def _():
+            pl.semaphore_signal(barrier, inc=1, device_id=(c, tm), device_id_type=MESH)
+
+    @pl.when(jnp.logical_not(last))
+    def _():
+        pl.semaphore_signal(barrier, inc=1, device_id=(me, tm + 1), device_id_type=MESH)
+
     get_record = pltpu.make_async_copy(record_hbm, record, load.at[0])
     get_fir = pltpu.make_async_copy(fir_hbm, fir, load.at[1])
     get_record.start()
     get_fir.start()
+    earlier = me + jnp.minimum(tm, 1)
+
+    @pl.when(earlier > 0)
+    def _():
+        pl.semaphore_wait(barrier, earlier)
+
+    @pl.when(jnp.logical_not(first))
+    def _():
+        pl.semaphore_signal(near, inc=1, device_id=(me, tm - 1), device_id_type=MESH)
+
     get_record.wait()
-    get_fir.wait()
-    pl.semaphore_wait(barrier, n + 1)
-
+    to_left = pltpu.make_async_remote_copy(
+        record.at[:, :HALO], high, halo_send.at[1], halo_recv.at[1],
+        device_id=(me, jnp.maximum(tm - 1, 0)), device_id_type=MESH,
+    )
     to_right = pltpu.make_async_remote_copy(
         record.at[:, length - HALO :], low, halo_send.at[0], halo_recv.at[0],
-        device_id=(me, right), device_id_type=MESH,
-    )
-    to_left = pltpu.make_async_remote_copy(
-        record.at[:, :HALO], high, halo_send.at[1], halo_recv.at[1],
-        device_id=(me, left), device_id_type=MESH,
-    )
-    to_right.start()
-    to_left.start()
-    to_right.wait_recv()
-    to_left.wait_recv()
-
-    before = jnp.where(tm > 0, low[...].astype(jnp.float32), 0.0)
-    after = jnp.where(tm < tn - 1, high[...].astype(jnp.float32), 0.0)
-    x = jnp.concatenate([before, record[...].astype(jnp.float32), after], axis=1)
+        device_id=(me, jnp.minimum(tm + 1, tn - 1)), device_id_type=MESH,
+    )
+
+    @pl.when(jnp.logical_not(first))
+    def _():
+        to_left.start()
+
+    for c in range(n - 1):
+        @pl.when(me > c)
+        def _():
+            pl.semaphore_signal(ready.at[me], inc=1, device_id=(c, tm), device_id_type=MESH)
+
+    @pl.when(jnp.logical_not(last))
+    def _():
+        pl.semaphore_wait(near, 1)
+        to_right.start()
+
+    get_fir.wait()
+
+    @pl.when(first)
+    def _():
+        low[...] = jnp.zeros_like(low)
+
+    @pl.when(last)
+    def _():
+        high[...] = jnp.zeros_like(high)
+
     half = (fir.shape[1] - 1) // 2
-    y = whiten(pltpu.roll(x, x.shape[1] - (HALO - MAXLAG - half), 1), fir[...], 0, SPAN)
+    edge = MAXLAG + half
+    taps = fir[...]
+    x = record[...].astype(jnp.float32)
+    x = jnp.concatenate([jnp.zeros((ch, HALO), jnp.float32), x, jnp.zeros((ch, HALO), jnp.float32)], axis=1)
+    y = whiten(pltpu.roll(x, x.shape[1] - (HALO - edge), 1), taps, SPAN + 128, SPAN)
+
+    @pl.when(jnp.logical_not(last))
+    def _():
+        to_left.wait_recv()
+
+    @pl.when(jnp.logical_not(first))
+    def _():
+        to_right.wait_recv()
+
+    column = lax.broadcasted_iota(jnp.int32, (ch, HALO), 1)
+    x = pltpu.roll(low[...].astype(jnp.float32), edge, 1)
+    x = jnp.where(column < edge, x, 0.0)
+    before = jnp.where(column < edge, whiten(x, taps, HALO, HALO), 0.0)
+    x = pltpu.roll(high[...].astype(jnp.float32), 2 * half, 1)
+    x = jnp.where((column >= 2 * half) & (column < 2 * half + edge), x, 0.0)
+    after = jnp.where(column < edge, whiten(x, taps, HALO, HALO), 0.0)
+    after = pltpu.roll(after, HALO - edge, 1)
+    y = jnp.concatenate(
+        [y[:, :HALO] + before, y[:, HALO : SPAN - HALO], y[:, SPAN - HALO :] + after], axis=1
+    )
     at = lax.broadcasted_iota(jnp.int32, y.shape, 1) + (tm * GROUP - MAXLAG)
     y = jnp.where((at >= 0) & (at < tn * GROUP), y, 0.0)
     y = y.astype(jnp.bfloat16).astype(jnp.float32)
     own[...] = pack(y)
 
-    copies = []
-    for d in range(1, n):
-        copy = pltpu.make_async_remote_copy(
-            own, blocks.at[me], send.at[d - 1], recv.at[me],
-            device_id=(lax.rem(me + d, n), tm), device_id_type=MESH,
+    copies = [
+        pltpu.make_async_remote_copy(
+            own, blocks.at[me], send.at[c], recv.at[me],
+            device_id=(c, tm), device_id_type=MESH,
         )
-        copy.start()
-        copies.append(copy)
+        for c in range(n)
+    ]
+    for c in range(n - 1):
+        @pl.when(me > c)
+        def _():
+            copies[c].start()
     blocks[me] = own[...]
 
     lead = jnp.concatenate(
@@ -103,21 +157,36 @@
         moved = pltpu.roll(line, 0, 1, stride=1, stride_axis=0)
         bands[i * MAXLAG : (i + 1) * MAXLAG, :] = moved.astype(jnp.bfloat16)
 
+    for c in range(1, n):
+        @pl.when(me < c)
+        def _():
+            pl.semaphore_wait(ready.at[c], 1)
+            copies[c].start()
+
     for c in range(n):
         @pl.when(me != c)
         def _():
             pltpu.make_async_remote_copy(
-                own, blocks.at[c], send.at[0], recv.at[c],
+                own, blocks.at[c], send.at[c], recv.at[c],
                 device_id=(c, tm), device_id_type=MESH,
             ).wait_recv()
 
         block = blocks[c].astype(jnp.float32)
         for k in range(SPAN // 128):
             wide[c * ch : (c + 1) * ch, k * 128 : (k + 1) * 128] = block[k * ch : (k + 1) * ch, :]
-    to_right.wait_send()
-    to_left.wait_send()
-    for copy in copies:
-        copy.wait_send()
+
+    @pl.when(jnp.logical_not(first))
+    def _():
+        to_left.wait_send()
+
+    @pl.when(jnp.logical_not(last))
+    def _():
+        to_right.wait_send()
+
+    for c in range(n):
+        @pl.when(me != c)
+        def _():
+            copies[c].wait_send()
 
 
 def correlate_kernel(wide, bands, out, result, sem):
@@ -170,8 +239,10 @@
             pltpu.SemaphoreType.DMA((2,)),
             pltpu.SemaphoreType.DMA((2,)),
             pltpu.SemaphoreType.DMA((2,)),
-            pltpu.SemaphoreType.DMA((n - 1,)),
             pltpu.SemaphoreType.DMA((n,)),
+            pltpu.SemaphoreType.DMA((n,)),
+            pltpu.SemaphoreType.REGULAR,
+            pltpu.SemaphoreType.REGULAR((n,)),
         ],
         compiler_params=pltpu.CompilerParams(
             collective_id=0, has_side_effects=True, vmem_limit_bytes=16 << 20

time: 15.1 us -> 12.8 us (0.85)
  the two profiles are of different devices: /device:TPU:0 before, /device:TPU:1 now
where the time goes in v3:
time: 12.8 us; the launch traced here: 12.5 us
  Pallas kernels  12.5 us (98%)
    pallas_call x1, Pallas kernels, local(): pl.pallas_call(gather_kernel, out_shape=(pltpu.VMEM((n * ch, SPAN), jnp.f...  10.9 us
    pallas_call x1, Pallas kernels, local(): pl.pallas_call(correlate_kernel, out_shape=jax.ShapeDtypeStruct((1, ch, n...  1.64 us

profile of v3, /device:TPU:1, one launch (start us, length us, event | category | flops | bytes accessed | tf_op | source)
XLA Modules:
  0.0 12.5 jit_solution(17240639435531566552)
XLA Ops:
  0.0 10.9 %shard_map.28 = (f32[96,768]{1,0:T(8,128)S(1)}, bf16[1536,640]{1,0:T(8,128)(2,1)S(1)}) custom-call(bf16[12,512]{1,0:T(8,128)(2,1)} %record_hbm.1, f32[12,65]{1,0:T(8,128)} %fir_hbm.1), custom_call_target="tpu_custom_call" | custom-call | tf_op jit(solution)/shard_map/pallas_call | solution.py:224
  10.9 1.6 %shard_map.29 = f32[1,12,96,256]{3,2,1,0:T(8,128)} custom-call(f32[96,768]{1,0:T(8,128)S(1)} %get-tuple-element.7.wide, bf16[1536,640]{1,0:T(8,128)(2,1)S(1)} %get-tuple-element.8.bands), custom_call_target="tpu_custom_call" | custom-call | tf_op jit(solution)/shard_map/pallas_call | solution.py:251

commit v4 on v3

--- a/solution.py
+++ b/solution.py
@@ -109,8 +109,10 @@
     edge = MAXLAG + half
     taps = fir[...]
     x = record[...].astype(jnp.float32)
-    x = jnp.concatenate([jnp.zeros((ch, HALO), jnp.float32), x, jnp.zeros((ch, HALO), jnp.float32)], axis=1)
-    y = whiten(pltpu.roll(x, x.shape[1] - (HALO - edge), 1), taps, SPAN + 128, SPAN)
+    x = jnp.concatenate([x, jnp.zeros((ch, MAXLAG), jnp.float32)], axis=1)
+    y = whiten(pltpu.roll(x, 2 * half, 1), taps, BAND, BAND)
+    y = jnp.concatenate([y, jnp.zeros((ch, MAXLAG), jnp.float32)], axis=1)
+    y = pltpu.roll(y, MAXLAG - half, 1)
 
     @pl.when(jnp.logical_not(last))
     def _():
@@ -206,11 +208,11 @@
                 result[2 * p + s, :, h * MAXLAG : (h + 1) * MAXLAG] = r[
                     h * rows : (h + 1) * rows, s * MAXLAG : (s + 1) * MAXLAG
                 ]
-        copy = pltpu.make_async_copy(
-            result.at[2 * p : 2 * p + 2], out.at[0, 2 * p : 2 * p + 2], sem.at[p]
-        )
-        copy.start()
-        copies.append(copy)
+            copy = pltpu.make_async_copy(
+                result.at[2 * p + s], out.at[0, 2 * p + s], sem.at[2 * p + s]
+            )
+            copy.start()
+            copies.append(copy)
     for copy in copies:
         copy.wait()
 
@@ -255,7 +257,7 @@
         out_specs=pl.BlockSpec(memory_space=pl.ANY),
         scratch_shapes=[
             pltpu.VMEM((ch, n * ch, LAGS), jnp.float32),
-            pltpu.SemaphoreType.DMA((ch // 2,)),
+            pltpu.SemaphoreType.DMA((ch,)),
         ],
         compiler_params=pltpu.CompilerParams(vmem_limit_bytes=16 << 20),
     )(wide, bands)

time: 12.8 us -> 12.8 us (level)
  no operation moved by 1% of the time
where the time goes in v4:
time: 12.8 us; the launch traced here: 12.6 us
  Pallas kernels  12.6 us (98%)
    pallas_call x1, Pallas kernels, local(): pl.pallas_call(gather_kernel, out_shape=(pltpu.VMEM((n * ch, SPAN), jnp.f...  10.9 us
    pallas_call x1, Pallas kernels, local(): pl.pallas_call(correlate_kernel, out_shape=jax.ShapeDtypeStruct((1, ch, n...  1.7 us

profile of v4, /device:TPU:1, one launch (start us, length us, event | category | flops | bytes accessed | tf_op | source)
XLA Modules:
  0.0 12.6 jit_solution(12682474127118541557)
XLA Ops:
  0.0 10.9 %shard_map.28 = (f32[96,768]{1,0:T(8,128)S(1)}, bf16[1536,640]{1,0:T(8,128)(2,1)S(1)}) custom-call(bf16[12,512]{1,0:T(8,128)(2,1)} %record_hbm.1, f32[12,65]{1,0:T(8,128)} %fir_hbm.1), custom_call_target="tpu_custom_call" | custom-call | tf_op jit(solution)/shard_map/pallas_call | solution.py:226
  10.9 1.7 %shard_map.29 = f32[1,12,96,256]{3,2,1,0:T(8,128)} custom-call(f32[96,768]{1,0:T(8,128)S(1)} %get-tuple-element.7.wide, bf16[1536,640]{1,0:T(8,128)(2,1)S(1)} %get-tuple-element.8.bands), custom_call_target="tpu_custom_call" | custom-call | tf_op jit(solution)/shard_map/pallas_call | solution.py:253

commit v5 on v4

--- a/solution.py
+++ b/solution.py
@@ -48,19 +48,19 @@
     first, last = tm == 0, tm == tn - 1
 
     barrier = pltpu.get_barrier_semaphore()
-    for c in range(1, n):
-        @pl.when(me < c)
-        def _():
-            pl.semaphore_signal(barrier, inc=1, device_id=(c, tm), device_id_type=MESH)
-
-    @pl.when(jnp.logical_not(last))
-    def _():
-        pl.semaphore_signal(barrier, inc=1, device_id=(me, tm + 1), device_id_type=MESH)
-
     get_record = pltpu.make_async_copy(record_hbm, record, load.at[0])
     get_fir = pltpu.make_async_copy(fir_hbm, fir, load.at[1])
     get_record.start()
     get_fir.start()
+    for c in range(1, n):
+        @pl.when(me < c)
+        def _():
+            pl.semaphore_signal(barrier, inc=1, device_id=(c, tm), device_id_type=MESH)
+
+    @pl.when(jnp.logical_not(last))
+    def _():
+        pl.semaphore_signal(barrier, inc=1, device_id=(me, tm + 1), device_id_type=MESH)
+
     earlier = me + jnp.minimum(tm, 1)
 
     @pl.when(earlier > 0)
@@ -70,6 +70,11 @@
     @pl.when(jnp.logical_not(first))
     def _():
         pl.semaphore_signal(near, inc=1, device_id=(me, tm - 1), device_id_type=MESH)
+
+    for c in range(n - 1):
+        @pl.when(me > c)
+        def _():
+            pl.semaphore_signal(ready.at[me], inc=1, device_id=(c, tm), device_id_type=MESH)
 
     get_record.wait()
     to_left = pltpu.make_async_remote_copy(
@@ -84,11 +89,6 @@
     @pl.when(jnp.logical_not(first))
     def _():
         to_left.start()
-
-    for c in range(n - 1):
-        @pl.when(me > c)
-        def _():
-            pl.semaphore_signal(ready.at[me], inc=1, device_id=(c, tm), device_id_type=MESH)
 
     @pl.when(jnp.logical_not(last))
     def _():

time: 12.8 us -> 12.8 us (level)
  no operation moved by 1% of the time
where the time goes in v5:
time: 12.8 us; the launch traced here: 12.6 us
  Pallas kernels  12.6 us (98%)
    pallas_call x1, Pallas kernels, local(): pl.pallas_call(gather_kernel, out_shape=(pltpu.VMEM((n * ch, SPAN), jnp.f...  10.9 us
    pallas_call x1, Pallas kernels, local(): pl.pallas_call(correlate_kernel, out_shape=jax.ShapeDtypeStruct((1, ch, n...  1.71 us

profile of v5, /device:TPU:1, one launch (start us, length us, event | category | flops | bytes accessed | tf_op | source)
XLA Modules:
  0.0 12.6 jit_solution(8622251599282424858)
XLA Ops:
  0.0 10.9 %shard_map.28 = (f32[96,768]{1,0:T(8,128)S(1)}, bf16[1536,640]{1,0:T(8,128)(2,1)S(1)}) custom-call(bf16[12,512]{1,0:T(8,128)(2,1)} %record_hbm.1, f32[12,65]{1,0:T(8,128)} %fir_hbm.1), custom_call_target="tpu_custom_call" | custom-call | tf_op jit(solution)/shard_map/pallas_call | solution.py:226
  10.9 1.7 %shard_map.29 = f32[1,12,96,256]{3,2,1,0:T(8,128)} custom-call(f32[96,768]{1,0:T(8,128)S(1)} %get-tuple-element.7.wide, bf16[1536,640]{1,0:T(8,128)(2,1)S(1)} %get-tuple-element.8.bands), custom_call_target="tpu_custom_call" | custom-call | tf_op jit(solution)/shard_map/pallas_call | solution.py:253
